TPU v7x, 128 devices: a whole 4x4x4 slice. The times are simulated.
128 devices in a mesh: slab: 4 (over z), brick: 32 (over y, x, core).
Axes of the slice: x: 4, y: 4, z: 4, core: 2. Of those that a mesh axis runs over, the one named last changes fastest.
Arguments:
- positions: float32 [4, 3, 65536], P('slab', None, 'brick'), may hold values from 0 to 1
- dest_brick: int32 [4, 65536], P('slab', 'brick'), may hold values from 0 to 31, as said below
- cell_local: int32 [4, 65536], P('slab', 'brick'), may hold values from 0 to 31
Outputs:
- rebuilt: float32 [4, 7, 65536], P('slab', None, 'brick')
Inputs may be any that keep to these rules, and one draw needn't show every extreme that they name: `dest_brick`: an atom held by brick b (columns b * 2048 to (b + 1) * 2048 - 1) goes to brick b, b + 1 or b - 1, periodic along the bricks. Of one brick's atoms at most 112 stay in one of its own cells and at most 8 go to one cell of each brick beside it; in every brick some cell receives exactly these numbers from all three, 128 atoms.
All inputs are finite; a program needn't handle non-finite values.
Results may differ from a plain program's by a relative error of at most 0.0003.
Values sent between devices are 32-bit elements; how exact they have to be, the bound alone decides.
A program may use at most 64 MiB of HBM per device.

v0:
```python
import math

import jax
import jax.numpy as jnp
from jax import lax
from jax.sharding import PartitionSpec as P

CX = 1
CY = 8
CZ = 4
CAP = 128
SIDE_MOST = 8
CELLS_DEV = 32


SIGMA_SQ = 0.8
SOFT_SQ = 0.64
EPSILON = 0.05
SENTINEL = 64.0


def passed_along(value, axis, steps):
    count = lax.axis_size(axis)
    pairs = [(source, (source + steps) % count) for source in range(count)]
    return lax.ppermute(value, axis, pairs)


def extended(block, sides, width):
    for axis, dim in sides:
        count = lax.axis_size(axis)
        forward = [(i, i + 1) for i in range(count - 1)]
        forward.append((count - 1, 0))
        backward = [(target, source) for source, target in forward]
        low = lax.ppermute(
            lax.slice_in_dim(block, block.shape[dim] - width, None, axis=dim), axis, forward
        )
        high = lax.ppermute(lax.slice_in_dim(block, 0, width, axis=dim), axis, backward)
        block = jnp.concatenate([low, block, high], axis=dim)
    return block


def prefix(shard, axis, combine, identity):
    count, mine = (lax.axis_size(axis), lax.axis_index(axis))
    everything = lax.all_gather(shard, axis)
    start = jnp.broadcast_to(jnp.asarray(identity, shard.dtype), shard.shape)

    def turn(k, before):
        reached = k < mine
        new = combine(before, everything[k])
        return jnp.where(reached, new, before)

    return lax.fori_loop(0, count, turn, start)


def from_behind(block, axis, distance):
    devices = range(lax.axis_size(axis))
    route = [(i - distance, i) for i in devices if i - distance in devices]
    return lax.ppermute(block, axis, route)


def pair_sums(own_cell, other_cell, offset, self_pair):
    delta_x = own_cell[0][..., :, None] - (other_cell[0][..., None, :] + offset[0])
    delta_y = own_cell[1][..., :, None] - (other_cell[1][..., None, :] + offset[1])
    delta_z = own_cell[2][..., :, None] - (other_cell[2][..., None, :] + offset[2])
    dist_sq = delta_x * delta_x + delta_y * delta_y + delta_z * delta_z
    inverse = 1.0 / (dist_sq + SOFT_SQ)
    ratio = SIGMA_SQ * inverse
    cube_term = ratio * ratio * ratio
    sixth_term = cube_term * cube_term
    well_value = 4.0 * (sixth_term - cube_term)
    slope_value = -4.0 * (6.0 * sixth_term - 3.0 * cube_term) * inverse
    margin = jnp.maximum(1.0 - dist_sq, 0.0)
    energy = well_value * margin * margin
    derive = slope_value * margin * margin - 2.0 * well_value * margin
    if self_pair:
        distinct = lax.broadcasted_iota(jnp.int32, (CAP, CAP), 0) != lax.broadcasted_iota(
            jnp.int32, (CAP, CAP), 1
        )
        energy = jnp.where(distinct, energy, 0.0)
        derive = jnp.where(distinct, derive, 0.0)
    factor = -2.0 * EPSILON * derive
    return jnp.stack(
        [
            jnp.sum(factor * delta_x, -1),
            jnp.sum(factor * delta_y, -1),
            jnp.sum(factor * delta_z, -1),
            0.5 * EPSILON * jnp.sum(energy, -1),
        ]
    )


def group_ranks(group_key, groups):
    row_count = group_key.shape[0]
    block_rows = math.gcd(row_count, 256)
    row_iota = lax.broadcasted_iota(jnp.int32, (block_rows, block_rows), 0)
    lower_ones = (row_iota > lax.broadcasted_iota(jnp.int32, (block_rows, block_rows), 1)).astype(
        jnp.bfloat16
    )
    labels = jnp.arange(groups, dtype=jnp.int32)

    def advance(counts, key_block):
        matches = key_block[:, None] == labels[None, :]
        one_hot = matches.astype(jnp.bfloat16)
        within = jnp.dot(lower_ones, one_hot, preferred_element_type=jnp.float32)
        ranked = jnp.sum(jnp.where(matches, within + counts[None, :], 0.0), axis=1)
        return (counts + jnp.sum(one_hot, axis=0, dtype=jnp.float32), ranked.astype(jnp.int32))

    counts, ranked = lax.scan(
        advance, jnp.zeros((groups,), jnp.float32), group_key.reshape(-1, block_rows)
    )
    return (ranked.reshape(row_count), counts.astype(jnp.int32))


def add_counts(earlier, later):
    return earlier + later


def place_rows(result, rows_in, first_global, count_rows, shard_first):
    column_ids = jnp.arange(rows_in.shape[1], dtype=jnp.int32)
    target_col = first_global + column_ids - shard_first
    usable = (column_ids < count_rows) & (target_col >= 0) & (target_col < result.shape[1])
    return result.at[:, jnp.where(usable, target_col, result.shape[1])].set(rows_in, mode="drop")


def body(positions, dest_brick, cell_local):
    brick_count = lax.axis_size("brick")
    brick_index = lax.axis_index("brick")
    atom_place = positions[0]
    target = dest_brick[0]
    cell_of = cell_local[0]
    atom_count = target.shape[0]
    side_slots = CELLS_DEV * SIDE_MOST
    grid_slots = CELLS_DEV * CAP
    bucket = (target - brick_index + 1) % brick_count
    slot_rank, counts = group_ranks(bucket * CELLS_DEV + cell_of, 3 * CELLS_DEV)
    own_counts = counts[CELLS_DEV : 2 * CELLS_DEV]

    def outgoing(bucket_id):
        slot_index = jnp.where(bucket == bucket_id, cell_of * SIDE_MOST + slot_rank, side_slots)
        return (
            jnp.full((3, side_slots), SENTINEL, jnp.float32)
            .at[:, slot_index]
            .set(atom_place, mode="drop")
        )

    from_left = passed_along(outgoing(2), "brick", 1)
    from_right = passed_along(outgoing(0), "brick", -1)
    own_index = jnp.where(bucket == 1, cell_of * CAP + slot_rank, grid_slots)
    cell_grid = (
        jnp.full((3, grid_slots), SENTINEL, jnp.float32)
        .at[:, own_index]
        .set(atom_place, mode="drop")
    )
    side_iota = jnp.arange(SIDE_MOST, dtype=jnp.int32)[None, :]
    cell_base = jnp.arange(CELLS_DEV, dtype=jnp.int32)[:, None] * CAP

    def arrive(grid_now, arrived, before):
        present = arrived[0].reshape(CELLS_DEV, SIDE_MOST) < 2.0
        landing = jnp.where(present, cell_base + before[:, None] + side_iota, grid_slots).reshape(
            -1
        )
        return (
            grid_now.at[:, landing].set(arrived, mode="drop"),
            jnp.sum(present.astype(jnp.int32), axis=1),
        )

    cell_grid, left_counts = arrive(cell_grid, from_left, own_counts)
    cell_grid, right_counts = arrive(cell_grid, from_right, own_counts + left_counts)
    cell_counts = own_counts + left_counts + right_counts
    padded = extended(cell_grid.reshape(3, CX, CY, CZ, CAP), (("slab", 3), ("brick", 1)), 1)

    def column_forces(column, running):
        place_x = column // CY
        place_y = column % CY
        own_cell = lax.dynamic_slice(padded, (0, place_x + 1, place_y, 1, 0), (3, 1, 1, CZ, CAP))[
            :, 0, 0
        ]
        summed = jnp.zeros((4, CZ, CAP), jnp.float32)
        for step_x in (-1, 0, 1):
            for step_y in (-1, 0, 1):
                near_y = (place_y + step_y) % CY
                for step_z in (-1, 0, 1):
                    other_cell = lax.dynamic_slice(
                        padded, (0, place_x + 1 + step_x, near_y, 1 + step_z, 0), (3, 1, 1, CZ, CAP)
                    )[:, 0, 0]
                    summed = summed + pair_sums(
                        own_cell,
                        other_cell,
                        (float(step_x), float(step_y), float(step_z)),
                        step_x == 0 and step_y == 0 and (step_z == 0),
                    )
        return lax.dynamic_update_slice(running, summed[:, None], (0, column, 0, 0))

    slot_terms = lax.fori_loop(
        0, CX * CY, column_forces, jnp.zeros((4, CX * CY, CZ, CAP), jnp.float32)
    )
    slot_terms = slot_terms.reshape(4, grid_slots)
    cell_start = jnp.cumsum(cell_counts) - cell_counts
    kept_total = jnp.sum(cell_counts)
    slot_iota = jnp.arange(CAP, dtype=jnp.int32)[None, :]
    filled = slot_iota < cell_counts[:, None]
    packed_index = jnp.where(filled, cell_start[:, None] + slot_iota, grid_slots).reshape(-1)
    records = jnp.concatenate([cell_grid, slot_terms], axis=0)
    packed = jnp.zeros((7, grid_slots), jnp.float32).at[:, packed_index].set(records, mode="drop")
    first_row = prefix(kept_total, "brick", add_counts, jnp.int32(0))
    shard_first = brick_index * atom_count
    result = place_rows(
        jnp.zeros((7, atom_count), jnp.float32), packed, first_row, kept_total, shard_first
    )
    summary = jnp.stack([first_row, kept_total]).astype(jnp.float32)
    left_rows, left_summary = from_behind((packed, summary), "brick", 1)
    right_rows, right_summary = from_behind((packed, summary), "brick", -1)
    result = place_rows(
        result,
        left_rows,
        left_summary[0].astype(jnp.int32),
        left_summary[1].astype(jnp.int32),
        shard_first,
    )
    result = place_rows(
        result,
        right_rows,
        right_summary[0].astype(jnp.int32),
        right_summary[1].astype(jnp.int32),
        shard_first,
    )
    return result[None]


def solution(mesh):
    return jax.shard_map(
        body,
        mesh=mesh,
        in_specs=(P("slab", None, "brick"), P("slab", "brick"), P("slab", "brick")),
        out_specs=P("slab", None, "brick"),
        check_vma=False,
    )
```

profile of v0, /device:TPU:8, one launch (start us, length us, event | category | flops | bytes accessed | tf_op | source)
XLA Modules:
  0.0 291.4 jit_solution(12845830288614102512)
XLA Ops:
  2.6 3.5 %while.49 = (s32[]{:T(128)}, f32[96]{0:T(128)S(1)}, s32[8,256]{1,0:T(8,128)S(1)}, s32[8,256]{1,0:T(8,128)S(1)}) while((s32[]{:T(128)}, f32[96]{0:T(128)S(1)}, s32[8,256]{1,0:T(8,128)S(1)}, s32[8,256]{1,0:T(8,128)S(1)}) %tuple.433), condition=%wide.region_3.4_spmd.clone.clone, body=%wide.region_0.3_spmd.clone.sunk.clone | while | flops 12935267 | bytes 11599 | solution.py:108
  8.7 6.2 %scatter_custom_fusion.1 = f32[3,256]{0,1:T(8,128)} fusion(s32[2048]{0:T(1024)S(1)} %bitcast.763, f32[2048,3]{1,0:T(8,128)S(1)} %copy.45, f32[]{:T(128)} %constant.447.clone.1), kind=kCustom, calls=%fused_computation.1026 | custom fusion | bytes 3076 | tf_op jit(solution)/shard_map/scatter | solution.py:143
  17.0 6.2 %scatter_custom_fusion = f32[3,256]{0,1:T(8,128)} fusion(s32[2048]{0:T(1024)S(1)} %bitcast.762, f32[2048,3]{1,0:T(8,128)S(1)} %copy.45, f32[]{:T(128)} %constant.447.clone.1), kind=kCustom, calls=%fused_computation.1028 | custom fusion | bytes 3076 | tf_op jit(solution)/shard_map/scatter | solution.py:143
  23.2 6.1 %scatter_custom_fusion.2 = f32[3,4096]{0,1:T(8,128)S(1)} fusion(s32[2048]{0:T(1024)S(1)} %bitcast.765, f32[2048,3]{1,0:T(8,128)S(1)} %copy.45, f32[]{:T(128)} %constant.447.clone.1), kind=kCustom, calls=%fused_computation.1006 | custom fusion | bytes 49156 | tf_op jit(solution)/shard_map/scatter | solution.py:152
  33.1 16.6 %all-reduce = s32[32]{0:T(128)S(1)} all-reduce(s32[32]{0:T(128)S(1)} %dynamic-update-slice), channel_id=1, replica_groups=mesh['slab'=4,'brick'=32] {'brick'}, use_global_device_ids=true, to_apply=%add | all-reduce | flops 32 | bytes 256
  49.6 37.5 %while.47 = (s32[]{:T(128)}, s32[]{:T(128)}, s32[]{:T(128)}, s32[32]{0:T(128)S(1)}) while((s32[]{:T(128)}, s32[]{:T(128)}, s32[]{:T(128)}, s32[32]{0:T(128)S(1)}) %tuple.436), condition=%wide.region_10.11_spmd.clone, body=%wide.region_9.10_spmd.sunk.clone | while | flops 5 | bytes 107 | solution.py:52
  89.8 5.8 %collective-permute-start.8 = (f32[2]{0:T(128)S(1)}, f32[2]{0:T(128)S(1)}, u32[]{:S(2)}, u32[]{:S(2)}) collective-permute-start(f32[2]{0:T(128)S(1)} %add_convert_fusion), channel_id=1, source_target_pairs={{1,0},{2,1},{3,2},{4,3},{5,4},{6,5},{7,6},{8,7},{9,8},{10,9},{11,1... | collective-permute-start | bytes 32 | tf_op jit(solution)/shard_map/ppermute | solution.py:58
  102.2 4.1 %collective-permute-start.3 = (f32[3,1,8,1,128]{4,3,2,1,0:T(1,128)S(1)}, f32[3,1,8,1,128]{4,3,2,1,0:T(1,128)S(1)}, u32[]{:S(2)}, u32[]{:S(2)}) collective-permute-start(f32[3,1,8,1,128]{4,3,2,1,0:T(1,128)S(1)} %get-tuple-element.645), channel_id=1, source_target_pairs={{32,0},{64,32},{96,64},{0,96},{33,1},{65,33},{97,65},{1,97},{34,2}... | collective-permute-start | bytes 36872 | tf_op jit(solution)/shard_map/ppermute | solution.py:37
  108.2 3.0 %collective-permute-done.2 = f32[3,1,8,1,128]{4,3,2,1,0:T(1,128)S(1)} collective-permute-done((f32[3,1,8,1,128]{4,3,2,1,0:T(1,128)S(1)}, f32[3,1,8,1,128]{4,3,2,1,0:T(1,128)S(1)}, u32[]{:S(2)}, u32[]{:S(2)}) %collective-permute-start.2) | collective-permute-done | bytes 12320 | tf_op jit(solution)/shard_map/ppermute | solution.py:34
  113.8 3.9 %collective-permute-done.4 = f32[3,1,8,6,128]{4,3,2,1,0:T(8,128)S(1)} collective-permute-done((f32[3,1,8,6,128]{4,3,2,1,0:T(8,128)S(1)}, f32[3,1,8,6,128]{4,3,2,1,0:T(8,128)S(1)}, u32[]{:S(2)}, u32[]{:S(2)}) %collective-permute-start.4) | collective-permute-done | bytes 73760 | tf_op jit(solution)/shard_map/ppermute | solution.py:34
  117.8 113.7 %while.48 = (s32[]{:T(128)}, f32[4,8,4,128]{3,2,1,0:T(4,128)S(1)}, f32[3,3,8,6,128]{4,3,2,1,0:T(8,128)S(1)}) while((s32[]{:T(128)}, f32[4,8,4,128]{3,2,1,0:T(4,128)S(1)}, f32[3,3,8,6,128]{4,3,2,1,0:T(8,128)S(1)}) %tuple.439), condition=%wide.region_124.125_spmd.clone, body=%wide.region_15.124_spmd.sunk.clone | while | flops 67592776 | bytes 1141572 | solution.py:194
  118.2 2.4 fusion.631
  120.7 2.4 fusion.632
  125.6 2.5 fusion.634
  128.1 2.4 fusion.635
  132.4 2.4 fusion.631
  134.9 2.4 fusion.632
  139.8 2.5 fusion.634
  142.3 2.4 fusion.635
  146.7 2.4 fusion.631
  149.1 2.4 fusion.632
  154.0 2.5 fusion.634
  156.5 2.4 fusion.635
  160.9 2.4 fusion.631
  163.3 2.4 fusion.632
  168.2 2.5 fusion.634
  170.7 2.4 fusion.635
  175.1 2.4 fusion.631
  177.5 2.4 fusion.632
  182.4 2.5 fusion.634
  184.9 2.4 fusion.635
  189.3 2.4 fusion.631
  191.7 2.4 fusion.632
  196.6 2.5 fusion.634
  199.2 2.4 fusion.635
  203.5 2.4 fusion.631
  205.9 2.4 fusion.632
  210.9 2.5 fusion.634
  213.4 2.4 fusion.635
  217.7 2.4 fusion.631
  220.2 2.4 fusion.632
  225.1 2.5 fusion.634
  227.6 2.4 fusion.635
  233.6 11.4 %scatter_custom_fusion.5 = f32[7,4096]{0,1:T(8,128)S(1)} fusion(s32[4096]{0:T(1024)S(1)} %bitcast.761, f32[4096,7]{1,0:T(8,128)} %copy.53, f32[]{:T(128)} %constant.441.clone.1), kind=kCustom, calls=%fused_computation.1008 | custom fusion | bytes 115200 | tf_op jit(solution)/shard_map/scatter | solution.py:204
  247.6 5.8 %collective-permute-start.9 = (f32[7,4096]{1,0:T(8,128)S(1)}, f32[7,4096]{1,0:T(8,128)S(1)}, u32[]{:S(2)}, u32[]{:S(2)}) collective-permute-start(f32[7,4096]{1,0:T(8,128)S(1)} %copy.54), channel_id=1, source_target_pairs={{1,0},{2,1},{3,2},{4,3},{5,4},{6,5},{7,6},{8,7},{9,8},{10,9},{11,1... | collective-permute-start | bytes 344072 | tf_op jit(solution)/shard_map/ppermute | solution.py:58
  253.4 11.1 %scatter_custom_fusion.6 = f32[7,2048]{0,1:T(8,128)S(1)} fusion(s32[4096]{0:T(1024)S(1)} %bitcast.760, f32[7,4096]{0,1:T(8,128)S(1)} %scatter_custom_fusion.5, f32[]{:T(128)} %constant.441.clone.1), kind=kCustom, calls=%fused_computation.1004 | custom fusion | bytes 2154500 | tf_op jit(solution)/shard_map/scatter | solution.py:122
  268.1 11.0 %scatter_fusion = f32[7,2048]{0,1:T(8,128)S(1)} fusion(f32[7,2048]{0,1:T(8,128)S(1)} %scatter_custom_fusion.6, s32[4096]{0:T(1024)S(1)} %bitcast.755, f32[4096,7]{1,0:T(8,128)S(1)} %copy.55), kind=kCustom, calls=%fused_computation.7 | custom fusion | bytes 360448 | tf_op jit(solution)/shard_map/scatter | solution.py:122
  279.1 11.3 %scatter_fusion.1 = f32[7,2048]{0,1:T(8,128)S(1)} fusion(f32[7,2048]{0,1:T(8,128)S(1)} %scatter_fusion, s32[4096]{0:T(1024)S(1)} %bitcast.756, f32[4096,7]{1,0:T(8,128)} %copy.57), kind=kCustom, calls=%fused_computation.8 | custom fusion | bytes 360448 | tf_op jit(solution)/shard_map/scatter | solution.py:122
  (307 shorter events, 87.1 us)
Async XLA Ops:
  6.1 23.2 %copy-start = (u32[128]{0:T(128)S(1)}, u32[128]{0:T(128)}, u32[]{:S(2)}) copy-start(u32[128]{0:T(128)} %constant.461) | copy-start | bytes 1540
  14.9 15.1 %collective-permute-start.1 = (f32[3,256]{0,1:T(8,128)}, f32[3,256]{0,1:T(8,128)S(1)}, u32[]{:S(2)}, u32[]{:S(2)}) collective-permute-start(f32[3,256]{0,1:T(8,128)} %scatter_custom_fusion.1), channel_id=1, source_target_pairs={{0,31},{1,0},{2,1},{3,2},{4,3},{5,4},{6,5},{7,6},{8,7},{9,8},{10,9... | collective-permute-start | bytes 9224 | tf_op jit(solution)/shard_map/ppermute | solution.py:25
  23.2 6.8 %collective-permute-start = (f32[3,256]{0,1:T(8,128)}, f32[3,256]{0,1:T(8,128)S(1)}, u32[]{:S(2)}, u32[]{:S(2)}) collective-permute-start(f32[3,256]{0,1:T(8,128)} %scatter_custom_fusion), channel_id=1, source_target_pairs={{0,1},{1,2},{2,3},{3,4},{4,5},{5,6},{6,7},{7,8},{8,9},{9,10},{10,1... | collective-permute-start | bytes 9224 | tf_op jit(solution)/shard_map/ppermute | solution.py:25
  87.9 18.5 %collective-permute-start.6 = (f32[2]{0:T(128)S(1)}, f32[2]{0:T(128)S(1)}, u32[]{:S(2)}, u32[]{:S(2)}) collective-permute-start(f32[2]{0:T(128)S(1)} %add_convert_fusion), channel_id=1, source_target_pairs={{0,1},{1,2},{2,3},{3,4},{4,5},{5,6},{6,7},{7,8},{8,9},{9,10},{10,1... | collective-permute-start | bytes 32 | tf_op jit(solution)/shard_map/ppermute | solution.py:58
  89.8 22.1 %collective-permute-start.8 = (f32[2]{0:T(128)S(1)}, f32[2]{0:T(128)S(1)}, u32[]{:S(2)}, u32[]{:S(2)}) collective-permute-start(f32[2]{0:T(128)S(1)} %add_convert_fusion), channel_id=1, source_target_pairs={{1,0},{2,1},{3,2},{4,3},{5,4},{6,5},{7,6},{8,7},{9,8},{10,9},{11,1... | collective-permute-start | bytes 32 | tf_op jit(solution)/shard_map/ppermute | solution.py:58
  102.2 6.0 %collective-permute-start.3 = (f32[3,1,8,1,128]{4,3,2,1,0:T(1,128)S(1)}, f32[3,1,8,1,128]{4,3,2,1,0:T(1,128)S(1)}, u32[]{:S(2)}, u32[]{:S(2)}) collective-permute-start(f32[3,1,8,1,128]{4,3,2,1,0:T(1,128)S(1)} %get-tuple-element.645), channel_id=1, source_target_pairs={{32,0},{64,32},{96,64},{0,96},{33,1},{65,33},{97,65},{1,97},{34,2}... | collective-permute-start | bytes 36872 | tf_op jit(solution)/shard_map/ppermute | solution.py:37
  106.3 4.9 %collective-permute-start.2 = (f32[3,1,8,1,128]{4,3,2,1,0:T(1,128)S(1)}, f32[3,1,8,1,128]{4,3,2,1,0:T(1,128)S(1)}, u32[]{:S(2)}, u32[]{:S(2)}) collective-permute-start(f32[3,1,8,1,128]{4,3,2,1,0:T(1,128)S(1)} %get-tuple-element.644), channel_id=1, source_target_pairs={{0,32},{32,64},{64,96},{96,0},{1,33},{33,65},{65,97},{97,1},{2,34}... | collective-permute-start | bytes 36872 | tf_op jit(solution)/shard_map/ppermute | solution.py:34
  111.3 2.5 collective-permute-start.5
  111.4 6.4 %collective-permute-start.4 = (f32[3,1,8,6,128]{4,3,2,1,0:T(8,128)S(1)}, f32[3,1,8,6,128]{4,3,2,1,0:T(8,128)S(1)}, u32[]{:S(2)}, u32[]{:S(2)}) collective-permute-start(f32[3,1,8,6,128]{4,3,2,1,0:T(8,128)S(1)} %pad_maximum_fusion.1), channel_id=1, source_target_pairs={{0,1},{1,2},{2,3},{3,4},{4,5},{5,6},{6,7},{7,8},{8,9},{9,10},{10,1... | collective-permute-start | bytes 221192 | tf_op jit(solution)/shard_map/ppermute | solution.py:34
  245.6 18.9 %collective-permute-start.7 = (f32[7,4096]{1,0:T(8,128)S(1)}, f32[7,4096]{1,0:T(8,128)}, u32[]{:S(2)}, u32[]{:S(2)}) collective-permute-start(f32[7,4096]{1,0:T(8,128)S(1)} %copy.54), channel_id=1, source_target_pairs={{0,1},{1,2},{2,3},{3,4},{4,5},{5,6},{6,7},{7,8},{8,9},{9,10},{10,1... | collective-permute-start | bytes 344072 | tf_op jit(solution)/shard_map/ppermute | solution.py:58
  247.6 18.5 %collective-permute-start.9 = (f32[7,4096]{1,0:T(8,128)S(1)}, f32[7,4096]{1,0:T(8,128)S(1)}, u32[]{:S(2)}, u32[]{:S(2)}) collective-permute-start(f32[7,4096]{1,0:T(8,128)S(1)} %copy.54), channel_id=1, source_target_pairs={{1,0},{2,1},{3,2},{4,3},{5,4},{6,5},{7,6},{8,7},{9,8},{10,9},{11,1... | collective-permute-start | bytes 344072 | tf_op jit(solution)/shard_map/ppermute | solution.py:58
where the time goes:
time: 292 us; the launch traced here: 291 us
  other arithmetic  120 us (41%)
  local copies, waits for them, and re-layouts  100 us (34%)
  starting transfers between devices  22.1 us (8%)
  loops' own time  21.2 us (7%)
  blocking collectives  16.6 us (6%)
  waiting for transfers between devices  7 us (2%)
    reduce_sum x48, other arithmetic, pair_sums(): jnp.sum(factor * delta_x, -1)  106 us
    scatter x3, local copies, waits for them, and re-layouts, place_rows(): result.at[:, jnp.where(usable, target_col, result.shape[1])]  33.5 us
    another operation x1, loops' own time, prefix(): return lax.fori_loop(0, count, turn, start)  18.9 us
    dynamic_slice x32, local copies, waits for them, and re-layouts, turn(): new = combine(before, everything[k])  18.5 us
    unnamed x1, blocking collectives  16.6 us
    ppermute x4, starting transfers between devices, from_behind(): return lax.ppermute(block, axis, route)  15.3 us
    scatter x2, local copies, waits for them, and re-layouts, outgoing(): return jnp.full((3, side_slots), SENTINEL, jnp.float32).at[:, slot_index]...  12.4 us
    scatter x2, local copies, waits for them, and re-layouts, body(): jnp.zeros((7, grid_slots), jnp.float32).at[:, packed_index]  12 us
  transfers between devices with their start and end apart: 10, of which 2 were waited for; matrix products, arithmetic and copies ran while one was open for 12% of the time, Pallas kernels for 0%

commit v1 on v0

--- a/solution.py
+++ b/solution.py
@@ -40,16 +40,10 @@
 
 
 def prefix(shard, axis, combine, identity):
-    count, mine = (lax.axis_size(axis), lax.axis_index(axis))
+    mine = lax.axis_index(axis)
     everything = lax.all_gather(shard, axis)
-    start = jnp.broadcast_to(jnp.asarray(identity, shard.dtype), shard.shape)
-
-    def turn(k, before):
-        reached = k < mine
-        new = combine(before, everything[k])
-        return jnp.where(reached, new, before)
-
-    return lax.fori_loop(0, count, turn, start)
+    lower = jnp.arange(everything.shape[0], dtype=jnp.int32) < mine
+    return jnp.sum(jnp.where(lower, everything, identity))
 
 
 def from_behind(block, axis, distance):

time: 292 us -> 256 us (0.88)
  loops' own time: 21.2 us -> 2.27 us
  local copies, waits for them, and re-layouts: 100 us -> 81.5 us
    another operation x1 -> x0, loops' own time: 18.9 us -> none  [prefix(): return lax.fori_loop(0, count, turn, start)]
    dynamic_slice x32 -> x0, local copies, waits for them, and re-layouts: 18.5 us -> none  [turn(): new = combine(before, everything[k])]
  transfers between devices with their start and end apart: 10 -> 10, of which waited for: 2 -> 2; matrix products, arithmetic and copies ran while one was open for 12% -> 13% of each run, Pallas kernels for 0% -> 0%
where the time goes in v1:
time: 256 us
  other arithmetic  122 us (48%)
  local copies, waits for them, and re-layouts  81.5 us (32%)
  starting transfers between devices  22.1 us (9%)
  blocking collectives  16.6 us (6%)
  waiting for transfers between devices  6.82 us (3%)
  between operations  2.93 us (1%)
    reduce_sum x48, other arithmetic, pair_sums(): jnp.sum(factor * delta_x, -1)  106 us
    scatter x3, local copies, waits for them, and re-layouts, place_rows(): result.at[:, jnp.where(usable, target_col, result.shape[1])]  33.5 us
    unnamed x1, blocking collectives  16.6 us
    ppermute x4, starting transfers between devices, from_behind(): return lax.ppermute(block, axis, route)  15.3 us
    scatter x2, local copies, waits for them, and re-layouts, outgoing(): return jnp.full((3, side_slots), SENTINEL, jnp.float32).at[:, slot_index]...  12.4 us
    scatter x2, local copies, waits for them, and re-layouts, body(): jnp.zeros((7, grid_slots), jnp.float32).at[:, packed_index]  12 us
    ppermute x2, waiting for transfers between devices, extended(): lax.ppermute(lax.slice_in_dim(block, block.shape[dim] - width, None, axis...  6.8 us
    scatter x1, local copies, waits for them, and re-layouts, body(): cell_grid = jnp.full((3, grid_slots), SENTINEL, jnp.float32).at[:, own_in...  6.09 us
  transfers between devices with their start and end apart: 10, of which 2 were waited for; matrix products, arithmetic and copies ran while one was open for 13% of the time, Pallas kernels for 0%

profile of v1, /device:TPU:8, one launch (start us, length us, event | category | flops | bytes accessed | tf_op | source)
XLA Modules:
  0.0 255.6 jit_solution(1931018266856976068)
XLA Ops:
  2.6 3.5 %while.34 = (s32[]{:T(128)}, f32[96]{0:T(128)S(1)}, s32[8,256]{1,0:T(8,128)S(1)}, s32[8,256]{1,0:T(8,128)S(1)}) while((s32[]{:T(128)}, f32[96]{0:T(128)S(1)}, s32[8,256]{1,0:T(8,128)S(1)}, s32[8,256]{1,0:T(8,128)S(1)}) %tuple.407), condition=%wide.region_3.4_spmd.clone.clone, body=%wide.region_0.3_spmd.clone.sunk.clone | while | flops 12935267 | bytes 11599 | solution.py:102
  8.7 6.2 %scatter_custom_fusion.1 = f32[3,256]{0,1:T(8,128)} fusion(s32[2048]{0:T(1024)S(1)} %bitcast.759, f32[2048,3]{1,0:T(8,128)S(1)} %copy.45, f32[]{:T(128)} %constant.426.clone.1), kind=kCustom, calls=%fused_computation.1026 | custom fusion | bytes 3076 | tf_op jit(solution)/shard_map/scatter | solution.py:137
  17.0 6.2 %scatter_custom_fusion = f32[3,256]{0,1:T(8,128)} fusion(s32[2048]{0:T(1024)S(1)} %bitcast.758, f32[2048,3]{1,0:T(8,128)S(1)} %copy.45, f32[]{:T(128)} %constant.426.clone.1), kind=kCustom, calls=%fused_computation.1028 | custom fusion | bytes 3076 | tf_op jit(solution)/shard_map/scatter | solution.py:137
  23.2 6.1 %scatter_custom_fusion.2 = f32[3,4096]{0,1:T(8,128)S(1)} fusion(s32[2048]{0:T(1024)S(1)} %bitcast.761, f32[2048,3]{1,0:T(8,128)S(1)} %copy.45, f32[]{:T(128)} %constant.426.clone.1), kind=kCustom, calls=%fused_computation.1006 | custom fusion | bytes 49156 | tf_op jit(solution)/shard_map/scatter | solution.py:146
  33.0 16.6 %all-reduce = s32[32]{0:T(128)S(1)} all-reduce(s32[32]{0:T(128)S(1)} %dynamic-update-slice), channel_id=1, replica_groups=mesh['slab'=4,'brick'=32] {'brick'}, use_global_device_ids=true, to_apply=%add | all-reduce | flops 32 | bytes 256
  53.4 5.8 %collective-permute-start.8 = (f32[2]{0:T(128)S(1)}, f32[2]{0:T(128)S(1)}, u32[]{:S(2)}, u32[]{:S(2)}) collective-permute-start(f32[2]{0:T(128)S(1)} %add_convert_fusion), channel_id=1, source_target_pairs={{1,0},{2,1},{3,2},{4,3},{5,4},{6,5},{7,6},{8,7},{9,8},{10,9},{11,1... | collective-permute-start | bytes 32 | tf_op jit(solution)/shard_map/ppermute | solution.py:52
  66.4 4.1 %collective-permute-start.3 = (f32[3,1,8,1,128]{4,3,2,1,0:T(1,128)S(1)}, f32[3,1,8,1,128]{4,3,2,1,0:T(1,128)S(1)}, u32[]{:S(2)}, u32[]{:S(2)}) collective-permute-start(f32[3,1,8,1,128]{4,3,2,1,0:T(1,128)S(1)} %get-tuple-element.557), channel_id=1, source_target_pairs={{32,0},{64,32},{96,64},{0,96},{33,1},{65,33},{97,65},{1,97},{34,2}... | collective-permute-start | bytes 36872 | tf_op jit(solution)/shard_map/ppermute | solution.py:37
  72.6 2.8 %collective-permute-done.2 = f32[3,1,8,1,128]{4,3,2,1,0:T(1,128)S(1)} collective-permute-done((f32[3,1,8,1,128]{4,3,2,1,0:T(1,128)S(1)}, f32[3,1,8,1,128]{4,3,2,1,0:T(1,128)S(1)}, u32[]{:S(2)}, u32[]{:S(2)}) %collective-permute-start.2) | collective-permute-done | bytes 12320 | tf_op jit(solution)/shard_map/ppermute | solution.py:34
  78.0 4.0 %collective-permute-done.4 = f32[3,1,8,6,128]{4,3,2,1,0:T(8,128)S(1)} collective-permute-done((f32[3,1,8,6,128]{4,3,2,1,0:T(8,128)S(1)}, f32[3,1,8,6,128]{4,3,2,1,0:T(8,128)S(1)}, u32[]{:S(2)}, u32[]{:S(2)}) %collective-permute-start.4) | collective-permute-done | bytes 73760 | tf_op jit(solution)/shard_map/ppermute | solution.py:34
  82.0 113.7 %while.33 = (s32[]{:T(128)}, f32[4,8,4,128]{3,2,1,0:T(4,128)S(1)}, f32[3,3,8,6,128]{4,3,2,1,0:T(8,128)S(1)}) while((s32[]{:T(128)}, f32[4,8,4,128]{3,2,1,0:T(4,128)S(1)}, f32[3,3,8,6,128]{4,3,2,1,0:T(8,128)S(1)}) %tuple.410), condition=%wide.region_123.124_spmd.clone, body=%wide.region_14.123_spmd.sunk.clone | while | flops 67592776 | bytes 1141572 | solution.py:188
  82.4 2.4 fusion.632
  84.9 2.4 fusion.633
  89.8 2.5 fusion.635
  92.3 2.4 fusion.636
  96.6 2.4 fusion.632
  99.1 2.4 fusion.633
  101.5 2.4 fusion.634
  104.0 2.5 fusion.635
  106.5 2.4 fusion.636
  110.9 2.4 fusion.632
  113.3 2.4 fusion.633
  118.2 2.5 fusion.635
  120.7 2.4 fusion.636
  125.1 2.4 fusion.632
  127.5 2.4 fusion.633
  132.4 2.5 fusion.635
  134.9 2.4 fusion.636
  139.3 2.4 fusion.632
  141.7 2.4 fusion.633
  146.6 2.5 fusion.635
  149.1 2.4 fusion.636
  153.5 2.4 fusion.632
  155.9 2.4 fusion.633
  160.8 2.5 fusion.635
  163.4 2.4 fusion.636
  167.7 2.4 fusion.632
  170.1 2.4 fusion.633
  175.1 2.5 fusion.635
  177.6 2.4 fusion.636
  181.9 2.4 fusion.632
  184.4 2.4 fusion.633
  189.3 2.5 fusion.635
  191.8 2.4 fusion.636
  197.8 11.4 %scatter_custom_fusion.5 = f32[7,4096]{0,1:T(8,128)S(1)} fusion(s32[4096]{0:T(1024)S(1)} %bitcast.757, f32[4096,7]{1,0:T(8,128)} %copy.53, f32[]{:T(128)} %constant.420.clone.1), kind=kCustom, calls=%fused_computation.1008 | custom fusion | bytes 115200 | tf_op jit(solution)/shard_map/scatter | solution.py:198
  211.8 5.8 %collective-permute-start.9 = (f32[7,4096]{1,0:T(8,128)S(1)}, f32[7,4096]{1,0:T(8,128)S(1)}, u32[]{:S(2)}, u32[]{:S(2)}) collective-permute-start(f32[7,4096]{1,0:T(8,128)S(1)} %copy.54), channel_id=1, source_target_pairs={{1,0},{2,1},{3,2},{4,3},{5,4},{6,5},{7,6},{8,7},{9,8},{10,9},{11,1... | collective-permute-start | bytes 344072 | tf_op jit(solution)/shard_map/ppermute | solution.py:52
  217.6 11.1 %scatter_custom_fusion.6 = f32[7,2048]{0,1:T(8,128)S(1)} fusion(s32[4096]{0:T(1024)S(1)} %bitcast.756, f32[7,4096]{0,1:T(8,128)S(1)} %scatter_custom_fusion.5, f32[]{:T(128)} %constant.420.clone.1), kind=kCustom, calls=%fused_computation.1004 | custom fusion | bytes 2154500 | tf_op jit(solution)/shard_map/scatter | solution.py:116
  232.3 11.0 %scatter_fusion = f32[7,2048]{0,1:T(8,128)S(1)} fusion(f32[7,2048]{0,1:T(8,128)S(1)} %scatter_custom_fusion.6, s32[4096]{0:T(1024)S(1)} %bitcast.751, f32[4096,7]{1,0:T(8,128)S(1)} %copy.55), kind=kCustom, calls=%fused_computation.7 | custom fusion | bytes 360448 | tf_op jit(solution)/shard_map/scatter | solution.py:116
  243.3 11.3 %scatter_fusion.1 = f32[7,2048]{0,1:T(8,128)S(1)} fusion(f32[7,2048]{0,1:T(8,128)S(1)} %scatter_fusion, s32[4096]{0:T(1024)S(1)} %bitcast.752, f32[4096,7]{1,0:T(8,128)} %copy.57), kind=kCustom, calls=%fused_computation.8 | custom fusion | bytes 360448 | tf_op jit(solution)/shard_map/scatter | solution.py:116
  (275 shorter events, 67.9 us)
Async XLA Ops:
  6.1 23.2 %copy-start = (u32[128]{0:T(128)S(1)}, u32[128]{0:T(128)}, u32[]{:S(2)}) copy-start(u32[128]{0:T(128)} %constant.440) | copy-start | bytes 1540
  14.9 15.1 %collective-permute-start.1 = (f32[3,256]{0,1:T(8,128)}, f32[3,256]{0,1:T(8,128)S(1)}, u32[]{:S(2)}, u32[]{:S(2)}) collective-permute-start(f32[3,256]{0,1:T(8,128)} %scatter_custom_fusion.1), channel_id=1, source_target_pairs={{0,31},{1,0},{2,1},{3,2},{4,3},{5,4},{6,5},{7,6},{8,7},{9,8},{10,9... | collective-permute-start | bytes 9224 | tf_op jit(solution)/shard_map/ppermute | solution.py:25
  23.2 6.8 %collective-permute-start = (f32[3,256]{0,1:T(8,128)}, f32[3,256]{0,1:T(8,128)S(1)}, u32[]{:S(2)}, u32[]{:S(2)}) collective-permute-start(f32[3,256]{0,1:T(8,128)} %scatter_custom_fusion), channel_id=1, source_target_pairs={{0,1},{1,2},{2,3},{3,4},{4,5},{5,6},{6,7},{7,8},{8,9},{9,10},{10,1... | collective-permute-start | bytes 9224 | tf_op jit(solution)/shard_map/ppermute | solution.py:25
  51.5 19.0 %collective-permute-start.6 = (f32[2]{0:T(128)S(1)}, f32[2]{0:T(128)S(1)}, u32[]{:S(2)}, u32[]{:S(2)}) collective-permute-start(f32[2]{0:T(128)S(1)} %add_convert_fusion), channel_id=1, source_target_pairs={{0,1},{1,2},{2,3},{3,4},{4,5},{5,6},{6,7},{7,8},{8,9},{9,10},{10,1... | collective-permute-start | bytes 32 | tf_op jit(solution)/shard_map/ppermute | solution.py:52
  53.4 22.6 %collective-permute-start.8 = (f32[2]{0:T(128)S(1)}, f32[2]{0:T(128)S(1)}, u32[]{:S(2)}, u32[]{:S(2)}) collective-permute-start(f32[2]{0:T(128)S(1)} %add_convert_fusion), channel_id=1, source_target_pairs={{1,0},{2,1},{3,2},{4,3},{5,4},{6,5},{7,6},{8,7},{9,8},{10,9},{11,1... | collective-permute-start | bytes 32 | tf_op jit(solution)/shard_map/ppermute | solution.py:52
  66.4 6.2 %collective-permute-start.3 = (f32[3,1,8,1,128]{4,3,2,1,0:T(1,128)S(1)}, f32[3,1,8,1,128]{4,3,2,1,0:T(1,128)S(1)}, u32[]{:S(2)}, u32[]{:S(2)}) collective-permute-start(f32[3,1,8,1,128]{4,3,2,1,0:T(1,128)S(1)} %get-tuple-element.557), channel_id=1, source_target_pairs={{32,0},{64,32},{96,64},{0,96},{33,1},{65,33},{97,65},{1,97},{34,2}... | collective-permute-start | bytes 36872 | tf_op jit(solution)/shard_map/ppermute | solution.py:37
  70.5 4.9 %collective-permute-start.2 = (f32[3,1,8,1,128]{4,3,2,1,0:T(1,128)S(1)}, f32[3,1,8,1,128]{4,3,2,1,0:T(1,128)S(1)}, u32[]{:S(2)}, u32[]{:S(2)}) collective-permute-start(f32[3,1,8,1,128]{4,3,2,1,0:T(1,128)S(1)} %get-tuple-element.556), channel_id=1, source_target_pairs={{0,32},{32,64},{64,96},{96,0},{1,33},{33,65},{65,97},{97,1},{2,34}... | collective-permute-start | bytes 36872 | tf_op jit(solution)/shard_map/ppermute | solution.py:34
  75.5 2.5 collective-permute-start.5
  75.6 6.4 %collective-permute-start.4 = (f32[3,1,8,6,128]{4,3,2,1,0:T(8,128)S(1)}, f32[3,1,8,6,128]{4,3,2,1,0:T(8,128)S(1)}, u32[]{:S(2)}, u32[]{:S(2)}) collective-permute-start(f32[3,1,8,6,128]{4,3,2,1,0:T(8,128)S(1)} %pad_maximum_fusion.1), channel_id=1, source_target_pairs={{0,1},{1,2},{2,3},{3,4},{4,5},{5,6},{6,7},{7,8},{8,9},{9,10},{10,1... | collective-permute-start | bytes 221192 | tf_op jit(solution)/shard_map/ppermute | solution.py:34
  209.8 18.9 %collective-permute-start.7 = (f32[7,4096]{1,0:T(8,128)S(1)}, f32[7,4096]{1,0:T(8,128)}, u32[]{:S(2)}, u32[]{:S(2)}) collective-permute-start(f32[7,4096]{1,0:T(8,128)S(1)} %copy.54), channel_id=1, source_target_pairs={{0,1},{1,2},{2,3},{3,4},{4,5},{5,6},{6,7},{7,8},{8,9},{9,10},{10,1... | collective-permute-start | bytes 344072 | tf_op jit(solution)/shard_map/ppermute | solution.py:52
  211.8 18.5 %collective-permute-start.9 = (f32[7,4096]{1,0:T(8,128)S(1)}, f32[7,4096]{1,0:T(8,128)S(1)}, u32[]{:S(2)}, u32[]{:S(2)}) collective-permute-start(f32[7,4096]{1,0:T(8,128)S(1)} %copy.54), channel_id=1, source_target_pairs={{1,0},{2,1},{3,2},{4,3},{5,4},{6,5},{7,6},{8,7},{9,8},{10,9},{11,1... | collective-permute-start | bytes 344072 | tf_op jit(solution)/shard_map/ppermute | solution.py:52
